TPU v7x, 256 devices: a whole 4x4x8 slice. The times are simulated.
256 devices in a mesh: head: 4 (over x), seq: 64 (over z, y, core).
Axes of the slice: x: 4, y: 4, z: 8, core: 2. Of those that a mesh axis runs over, the one named last changes fastest.
Arguments:
- queries: bfloat16 [16384, 3072], P(('head', 'seq')), may hold values from -6 to 6
- key_rows: bfloat16 [49152, 3072], P('seq', 'head'), may hold values from -6 to 6
- values: bfloat16 [49152, 3072], P('seq', 'head'), may hold values from -6 to 6
- w_out: bfloat16 [3072, 6144], P('head'), may hold values from -1.1953125 to 1.1953125
- picked: int32 [256, 24], replicated, may hold values from 0 to 767, as said below
- counts: int32 [256], replicated, may hold values from 8 to 24
- tile_home: int32 [768], replicated, may hold values from 0 to 767, as said below
Outputs:
- layer_out: bfloat16 [16384, 6144], P(('head', 'seq'))
Inputs may be any that keep to these rules, and one draw needn't show every extreme that they name: `picked`: query tiles j with the same j modulo the number of devices along seq form a group. The used entries of one group are distinct key tiles; key tile t is stored on owner tile_home[t] // 12, and at most 2 used entries of one group are stored on one owner, exactly 2 for some owner in every group. `tile_home`: A permutation of the key tiles.
All inputs are finite; a program needn't handle non-finite values.
Results may differ from a plain program's by a relative error of at most 0.009.
Values may be sent and summed in bfloat16 or wider, within the bound.
No kernel may reach another device: no remote copies, remote signals or barrier semaphores. Data moves between devices by JAX's collectives and lax.ppermute only.
A program may use at most 128 MiB of HBM per device.

v0:
```python
import jax
import jax.numpy as jnp
from jax import lax
from jax.sharding import PartitionSpec as P

HD = 128
MAXSEL = 24


def body(queries, key_rows, values, w_out, picked, counts, tile_home):
    head_count = lax.axis_size("head")
    seq_count = lax.axis_size("seq")
    seq_index = lax.axis_index("seq")
    tile_rows = queries.shape[0]
    width_local = w_out.shape[0]
    heads_local = width_local // HD
    tiles_dev = key_rows.shape[0] // tile_rows
    capacity = max(2, head_count * MAXSEL // seq_count)
    request_count = head_count * MAXSEL
    local_queries = lax.all_to_all(queries, "head", split_axis=1, concat_axis=0, tiled=True)
    group_pick = (
        picked.reshape(head_count, seq_count, MAXSEL)
        .transpose(1, 0, 2)
        .reshape(seq_count, request_count)
    )
    group_count = counts.reshape(head_count, seq_count).transpose(1, 0)
    position = lax.broadcasted_iota(jnp.int32, (head_count, MAXSEL), 1).reshape(request_count)
    is_live = position[None, :] < jnp.repeat(group_count, MAXSEL, axis=1)
    stored = tile_home[group_pick]
    owner_of = stored // tiles_dev
    inside_offset = stored % tiles_dev
    owner_ids = lax.broadcasted_iota(jnp.int32, (1, 1, seq_count), 2)
    hit_table = ((owner_of[:, :, None] == owner_ids) & is_live[:, :, None]).astype(jnp.int32)
    before = jnp.cumsum(hit_table, axis=1) - hit_table
    slot_rank = jnp.sum(before * hit_table, axis=2)
    for_me = (owner_of == seq_index) & is_live
    slot_ids = lax.broadcasted_iota(jnp.int32, (1, 1, capacity), 2)
    slot_hits = (for_me[:, :, None] & (slot_rank[:, :, None] == slot_ids)).astype(jnp.int32)
    send_within = jnp.sum(slot_hits * inside_offset[:, :, None], axis=1)
    key_blocks = key_rows.reshape(tiles_dev, tile_rows, width_local)
    value_blocks = values.reshape(tiles_dev, tile_rows, width_local)
    send_keys = key_blocks[send_within]
    send_values = value_blocks[send_within]
    my_owner = lax.dynamic_index_in_dim(owner_of, seq_index, 0, keepdims=False)
    my_rank = lax.dynamic_index_in_dim(slot_rank, seq_index, 0, keepdims=False)
    my_live = lax.dynamic_index_in_dim(is_live, seq_index, 0, keepdims=False)
    flat_slot = my_owner * capacity + jnp.minimum(my_rank, capacity - 1)

    def arrange(incoming_rows):
        picked_rows = incoming_rows.reshape(seq_count * capacity, tile_rows, width_local)[flat_slot]
        return picked_rows.reshape(head_count, MAXSEL * tile_rows, heads_local, HD)

    query_heads = local_queries.reshape(head_count, tile_rows, heads_local, HD)
    key_live = jnp.repeat(my_live.reshape(head_count, MAXSEL), tile_rows, axis=1)[:, None, None, :]
    recv_keys, recv_values = (
        lax.all_to_all(send_keys, "seq", split_axis=0, concat_axis=0, tiled=True),
        lax.all_to_all(send_values, "seq", split_axis=0, concat_axis=0, tiled=True),
    )
    logit_scores = jnp.einsum(
        "rqhd,rkhd->rhqk", query_heads, arrange(recv_keys), preferred_element_type=jnp.float32
    ) * HD ** (-0.5)
    logit_scores = jnp.where(key_live, logit_scores, -1e30)
    row_top = jnp.max(logit_scores, axis=-1, keepdims=True)
    exponent = jnp.where(key_live, jnp.exp(logit_scores - row_top), 0.0)
    weights = exponent.astype(jnp.bfloat16)
    row_sum_total = jnp.sum(exponent, axis=-1)
    fetched_values = arrange(recv_values)
    mixed = jnp.einsum(
        "rhqk,rkhd->rqhd", weights, fetched_values, preferred_element_type=jnp.float32
    )
    mixed = mixed / jnp.transpose(row_sum_total, (0, 2, 1))[:, :, :, None]
    attended = mixed.astype(jnp.bfloat16).reshape(head_count * tile_rows, width_local)
    partial_sum = jnp.dot(attended, w_out, preferred_element_type=jnp.float32)
    summed = lax.psum(partial_sum.astype(jnp.bfloat16), "head").astype(jnp.float32)
    layer_out = lax.dynamic_slice_in_dim(summed, lax.axis_index("head") * tile_rows, tile_rows, 0)
    return layer_out.astype(jnp.bfloat16)


def solution(mesh):
    placed = (
        P(("head", "seq"), None),
        P("seq", "head"),
        P("seq", "head"),
        P("head", None),
        P(),
        P(),
        P(),
    )
    return jax.shard_map(
        body, mesh=mesh, in_specs=placed, out_specs=P(("head", "seq"), None), check_vma=False
    )
```

profile of v0, /device:TPU:1, one launch (start us, length us, event | category | flops | bytes accessed | tf_op | source)
XLA Modules:
  0.0 815.5 jit_solution(14306597630840057382)
XLA Ops:
  6.5 0.9 reshape.182
  7.5 0.1 copy.52
  7.6 0.1 reshape.196
  7.7 0.0 copy-start.5
  7.7 24.8 %gather_fusion = s32[6144]{0:T(1024)S(1)} fusion(s32[768]{0:T(1024)S(1)} %copy-done.2, s32[6144]{0:T(1024)S(1)} %broadcast_clamp_fusion), kind=kCustom, calls=%fused_computation | custom fusion | bytes 73728 | tf_op jit(solution)/shard_map/gather | solution.py:29
  32.5 0.1 reshape.239
  32.6 0.1 copy.53
  32.7 0.1 reshape.241
  32.8 0.1 copy.55
  32.9 0.1 reshape.243
  33.0 0.1 copy.54
  33.1 0.1 lt.73
  33.2 0.1 reshape.184
  33.3 0.1 compare_and_fusion
  33.4 4.9 fusion.17
  38.3 0.1 copy.58
  38.4 0.1 copy.57
  38.5 0.1 copy.62
  38.6 0.1 select_reduce_fusion
  38.7 0.1 copy.63
  38.8 0.1 reshape.204
  39.0 8.3 %gather_fusion.3 = bf16[128,64,768]{2,1,0:T(8,128)(2,1)} fusion(bf16[12,64,768]{2,1,0:T(8,128)(2,1)S(1)} %bitcast.64, s32[1024]{0:T(1024)S(1)} %pad_clamp_fusion.1), kind=kCustom, calls=%fused_computation.3 | custom fusion | bytes 25166336 | tf_op jit(solution)/shard_map/gather | solution.py:42
  47.3 13.3 %all-to-all-start.1 = ((bf16[64,2,64,768]{3,2,1,0:T(8,128)(2,1)}), bf16[64,2,64,768]{3,2,1,0:T(8,128)(2,1)}, u32[]{:S(2)}, u32[]{:S(2)}) async-start(bf16[64,2,64,768]{3,2,1,0:T(8,128)(2,1)} %bitcast.67), calls=%async_computation.1 | async-start | bytes 25165824 | tf_op jit(solution)/shard_map/all_to_all | solution.py:56
  60.6 8.3 %gather_fusion.1 = bf16[128,64,768]{2,1,0:T(8,128)(2,1)} fusion(bf16[12,64,768]{2,1,0:T(8,128)(2,1)S(1)} %bitcast.65, s32[1024]{0:T(1024)S(1)} %pad_clamp_fusion.1), kind=kCustom, calls=%fused_computation.1 | custom fusion | bytes 25166336 | tf_op jit(solution)/shard_map/gather | solution.py:43
  68.9 263.8 %all-to-all-done.1 = bf16[64,2,64,768]{3,2,1,0:T(8,128)(2,1)} async-done(((bf16[64,2,64,768]{3,2,1,0:T(8,128)(2,1)}), bf16[64,2,64,768]{3,2,1,0:T(8,128)(2,1)}, u32[]{:S(2)}, u32[]{:S(2)}) %all-to-all-start.1) | async-done | bytes 12582944 | tf_op jit(solution)/shard_map/all_to_all | solution.py:56
  332.7 14.5 %all-to-all-start = ((bf16[64,2,64,768]{3,2,1,0:T(8,128)(2,1)}), bf16[64,2,64,768]{3,2,1,0:T(8,128)(2,1)}, u32[]{:S(2)}, u32[]{:S(2)}) async-start(bf16[64,2,64,768]{3,2,1,0:T(8,128)(2,1)} %bitcast.66), calls=%async_computation | async-start | bytes 25165824 | tf_op jit(solution)/shard_map/all_to_all | solution.py:57
  347.2 0.8 copy.91
  348.0 0.2 dynamic-slice_reduce_fusion
  348.2 0.1 reshape.188
  348.3 0.1 broadcast_in_dim.41
  348.4 0.1 broadcast_in_dim.42
  348.5 0.2 add_reduce_fusion
  348.7 272.2 %all-to-all-done = bf16[64,2,64,768]{3,2,1,0:T(8,128)(2,1)} async-done(((bf16[64,2,64,768]{3,2,1,0:T(8,128)(2,1)}), bf16[64,2,64,768]{3,2,1,0:T(8,128)(2,1)}, u32[]{:S(2)}, u32[]{:S(2)}) %all-to-all-start) | async-done | bytes 12582944 | tf_op jit(solution)/shard_map/all_to_all | solution.py:57
  620.8 4.0 all-to-all-start.2
  624.9 12.0 %gather_fusion.4 = bf16[96,64,768]{2,1,0:T(8,128)(2,1)} fusion(bf16[128,64,768]{2,1,0:T(8,128)(2,1)} %bitcast.12, s32[1024]{0:T(1024)S(1)} %pad_clamp_fusion), kind=kCustom, calls=%fused_computation.4 | custom fusion | bytes 18874752 | tf_op jit(solution)/shard_map/gather | solution.py:50
  636.9 20.2 %reshape.191 = bf16[4,1536,6,128]{3,2,1,0:T(8,128)(2,1)} reshape(bf16[96,64,768]{2,1,0:T(8,128)(2,1)} %gather_fusion.4) | data formatting | bytes 18874368 | tf_op jit(solution)/shard_map/reshape | solution.py:51
  657.1 12.0 %gather_fusion.2 = bf16[96,64,768]{2,1,0:T(8,128)(2,1)} fusion(bf16[128,64,768]{2,1,0:T(8,128)(2,1)} %bitcast.8, s32[1024]{0:T(1024)S(1)} %pad_clamp_fusion), kind=kCustom, calls=%fused_computation.2 | custom fusion | bytes 18874752 | tf_op jit(solution)/shard_map/gather | solution.py:50
  669.1 20.2 %reshape.187 = bf16[4,1536,6,128]{3,2,1,0:T(8,128)(2,1)} reshape(bf16[96,64,768]{2,1,0:T(8,128)(2,1)} %gather_fusion.2) | data formatting | bytes 18874368 | tf_op jit(solution)/shard_map/reshape | solution.py:51
  689.2 0.0 all-to-all-done.2
  689.2 11.5 %fusion.6 = f32[4,6,1536,64]{2,3,1,0:T(8,128)} fusion(bf16[4,1536,6,128]{3,2,1,0:T(8,128)(2,1)} %reshape.191, bf16[64,4,768]{2,0,1:T(8,128)(2,1)S(1)} %all-to-all-done.2), kind=kOutput, calls=%fused_computation.13 | convolution fusion | flops 603979776 | bytes 19267584 | tf_op jit(solution)/shard_map/rqhd,rkhd->rhqk/dot_general | solution.py:59
  700.8 10.0 %fusion.45 = (f32[4,6,64]{2,1,0:T(8,128)S(1)}, bf16[4,6,64,1536]{3,2,1,0:T(8,128)(2,1)S(1)}) fusion(f32[4,6,1536,64]{2,3,1,0:T(8,128)} %fusion.6, pred[4,1536]{1,0:T(4,128)(4,1)S(1)} %broadcast_in_dim.42), kind=kOutput, calls=%fused_computation.61 | output fusion | flops 18875904 | bytes 14168064 | tf_op jit(solution)/shard_map/sub | solution.py:64
  710.8 7.5 fusion.32
  718.3 0.3 copy.68
  718.6 0.0 copy-start.1
  718.6 4.0 convolution_convert_fusion
  722.7 0.0 all-reduce.2.cloned.1.call-update
  722.7 83.8 %all-reduce.2.cloned.1.call-done = bf16[256,6144]{1,0:T(8,128)(2,1)} async-done(((bf16[256,6144]{1,0:T(8,128)(2,1)}), bf16[256,6144]{1,0:T(8,128)(2,1)}) %all-reduce.2.cloned.1.call-update) | async-done | bytes 3145744 | tf_op jit(solution)/shard_map/psum | solution.py:74
  806.5 2.1 convert_convert_fusion
  (29 shorter events, 0.1 us)
Async XLA Ops:
  6.5 32.5 %copy-start = (bf16[768,768]{1,0:T(8,128)(2,1)S(1)}, bf16[768,768]{1,0:T(8,128)(2,1)}, u32[]{:S(2)}) copy-start(bf16[768,768]{1,0:T(8,128)(2,1)} %param.8) | copy-start | bytes 3538948
  6.5 1.2 copy-start.2
  7.7 25.5 %copy-start.5 = (s32[256]{0:T(256)S(1)}, s32[256]{0:T(256)}, u32[]{:S(2)}) copy-start(s32[256]{0:T(256)} %param.12) | copy-start | bytes 3076
  47.3 13.4 %copy-start.3 = (bf16[768,768]{1,0:T(8,128)(2,1)S(1)}, bf16[768,768]{1,0:T(8,128)(2,1)}, u32[]{:S(2)}) copy-start(bf16[768,768]{1,0:T(8,128)(2,1)} %param.9) | copy-start | bytes 3538948
  47.3 285.5 %all-to-all-start.1 = ((bf16[64,2,64,768]{3,2,1,0:T(8,128)(2,1)}), bf16[64,2,64,768]{3,2,1,0:T(8,128)(2,1)}, u32[]{:S(2)}, u32[]{:S(2)}) async-start(bf16[64,2,64,768]{3,2,1,0:T(8,128)(2,1)} %bitcast.67), calls=%async_computation.1 | async-start | bytes 25165824 | tf_op jit(solution)/shard_map/all_to_all | solution.py:56
  332.7 14.5 %copy-start.4 = (bf16[64,3072]{1,0:T(8,128)(2,1)S(1)}, bf16[64,3072]{1,0:T(8,128)(2,1)}, u32[]{:S(2)}) copy-start(bf16[64,3072]{1,0:T(8,128)(2,1)} %param.7) | copy-start | bytes 1179652
  332.7 288.1 %all-to-all-start = ((bf16[64,2,64,768]{3,2,1,0:T(8,128)(2,1)}), bf16[64,2,64,768]{3,2,1,0:T(8,128)(2,1)}, u32[]{:S(2)}, u32[]{:S(2)}) async-start(bf16[64,2,64,768]{3,2,1,0:T(8,128)(2,1)} %bitcast.66), calls=%async_computation | async-start | bytes 25165824 | tf_op jit(solution)/shard_map/all_to_all | solution.py:57
  620.8 68.4 %all-to-all-start.2 = ((bf16[64,4,768]{2,0,1:T(8,128)(2,1)}), bf16[64,4,768]{2,0,1:T(8,128)(2,1)S(1)}, u32[]{:S(2)}, u32[]{:S(2)}) async-start(bf16[64,4,768]{2,0,1:T(8,128)(2,1)} %bitcast.63), calls=%async_computation.2 | async-start | bytes 786432 | tf_op jit(solution)/shard_map/all_to_all | solution.py:20
  624.8 181.7 %all-reduce.2.cloned.1.call-start = ((), (), s32[]{:S(2)}) async-start(), calls=%async_computation.3 | async-start | bytes 6291456 | tf_op jit(solution)/shard_map/psum | solution.py:74
  700.8 17.8 %slice-start = ((s8[9437184]{0:T(1024)(128)(4,1)}), s8[1048576]{0:T(1024)(128)(4,1)S(1)}, s32[]{:S(2)}) async-start(s8[9437184]{0:T(1024)(128)(4,1)} %bitcast.71), calls=%async_computation.4 | async-start | bytes 2097152
  700.8 17.8 %slice-start.1 = ((s8[9437184]{0:T(1024)(128)(4,1)}), s8[4194304]{0:T(1024)(128)(4,1)S(1)}, s32[]{:S(2)}) async-start(s8[9437184]{0:T(1024)(128)(4,1)} %bitcast.71), calls=%async_computation.5 | async-start | bytes 8388608
  710.8 7.8 slice-start.2
  718.6 90.0 %copy-start.1 = (bf16[768,768]{1,0:T(8,128)(2,1)S(1)}, bf16[768,768]{1,0:T(8,128)(2,1)}, u32[]{:S(2)}) copy-start(bf16[768,768]{1,0:T(8,128)(2,1)} %param.8) | copy-start | bytes 3538948
Sparse Core Ops, SparseCore 0:
  722.8 83.6 all-reduce.1
where the time goes:
time: 817 us; the launch traced here: 815 us
  waiting for transfers between devices  620 us (76%)
  local copies, waits for them, and re-layouts  110 us (13%)
  starting transfers between devices  31.8 us (4%)
  matrix products  23 us (3%)
  other arithmetic  17.5 us (2%)
  between operations  13.7 us (2%)
    all_to_all x1, waiting for transfers between devices, body(): lax.all_to_all(send_values, 'seq', split_axis=0, concat_axis=0, tiled=True)  272 us
    all_to_all x1, waiting for transfers between devices, body(): lax.all_to_all(send_keys, 'seq', split_axis=0, concat_axis=0, tiled=True)  264 us
    psum x1, waiting for transfers between devices, body(): lax.psum(partial_sum.astype(jnp.bfloat16), 'head').astype(jnp.float32)  83.8 us
    reshape x2, local copies, waits for them, and re-layouts, arrange(): return picked_rows.reshape(head_count, MAXSEL * tile_rows, heads_local, HD)  40.3 us
    gather x1, local copies, waits for them, and re-layouts, body(): stored = tile_home[group_pick]  24.8 us
    gather x2, local copies, waits for them, and re-layouts, arrange(): incoming_rows.reshape(seq_count * capacity, tile_rows, width_local)  24 us
  transfers between devices with their start and end apart: 4, of which 3 were waited for; matrix products, arithmetic and copies ran while one was open for 9% of the time, Pallas kernels for 0%

commit v1 on v0

--- a/solution.py
+++ b/solution.py
@@ -71,7 +71,9 @@
     mixed = mixed / jnp.transpose(row_sum_total, (0, 2, 1))[:, :, :, None]
     attended = mixed.astype(jnp.bfloat16).reshape(head_count * tile_rows, width_local)
     partial_sum = jnp.dot(attended, w_out, preferred_element_type=jnp.float32)
-    summed = lax.psum(partial_sum.astype(jnp.bfloat16), "head").astype(jnp.float32)
+    summed = jnp.sum(lax.all_gather(partial_sum.astype(jnp.bfloat16), "head"), axis=0).astype(
+        jnp.float32
+    )
     layer_out = lax.dynamic_slice_in_dim(summed, lax.axis_index("head") * tile_rows, tile_rows, 0)
     return layer_out.astype(jnp.bfloat16)
 

time: 817 us -> 867 us (1.061)
  waiting for transfers between devices: 620 us -> 660 us
  other arithmetic: 17.5 us -> 27 us
    all_gather x0 -> x1, waiting for transfers between devices: none -> 124 us  [body(): lax.all_gather(partial_sum.astype(jnp.bfloat16), 'head')]
    psum x1 -> x0, waiting for transfers between devices: 83.8 us -> none  [body(): lax.psum(partial_sum.astype(jnp.bfloat16), 'head').astype(jnp.float32)]
    reduce_sum x0 -> x1, other arithmetic: none -> 9.49 us  [body(): jnp.sum(lax.all_gather(partial_sum.astype(jnp.bfloat16), 'head'), axis=0)]
where the time goes in v1:
time: 867 us; the launch traced here: 865 us
  waiting for transfers between devices  660 us (76%)
  local copies, waits for them, and re-layouts  110 us (13%)
  starting transfers between devices  31.8 us (4%)
  other arithmetic  27 us (3%)
  matrix products  23.1 us (3%)
  between operations  13.7 us (2%)
    all_to_all x1, waiting for transfers between devices, body(): lax.all_to_all(send_values, 'seq', split_axis=0, concat_axis=0, tiled=True)  272 us
    all_to_all x1, waiting for transfers between devices, body(): lax.all_to_all(send_keys, 'seq', split_axis=0, concat_axis=0, tiled=True)  264 us
    all_gather x1, waiting for transfers between devices, body(): lax.all_gather(partial_sum.astype(jnp.bfloat16), 'head')  124 us
    reshape x2, local copies, waits for them, and re-layouts, arrange(): return picked_rows.reshape(head_count, MAXSEL * tile_rows, heads_local, HD)  40.3 us
    gather x1, local copies, waits for them, and re-layouts, body(): stored = tile_home[group_pick]  24.8 us
    gather x2, local copies, waits for them, and re-layouts, arrange(): incoming_rows.reshape(seq_count * capacity, tile_rows, width_local)  24 us
  transfers between devices with their start and end apart: 4, of which 3 were waited for; matrix products, arithmetic and copies ran while one was open for 9% of the time, Pallas kernels for 0%

profile of v1, /device:TPU:1, one launch (start us, length us, event | category | flops | bytes accessed | tf_op | source)
XLA Modules:
  0.0 865.2 jit_solution(17578803365170616030)
XLA Ops:
  6.5 0.9 reshape.182
  7.5 0.1 copy.52
  7.6 0.1 reshape.196
  7.7 0.0 copy-start.5
  7.7 24.8 %gather_fusion = s32[6144]{0:T(1024)S(1)} fusion(s32[768]{0:T(1024)S(1)} %copy-done.2, s32[6144]{0:T(1024)S(1)} %broadcast_clamp_fusion), kind=kCustom, calls=%fused_computation | custom fusion | bytes 73728 | tf_op jit(solution)/shard_map/gather | solution.py:29
  32.5 0.1 reshape.240
  32.6 0.1 copy.53
  32.7 0.1 reshape.242
  32.8 0.1 copy.55
  32.9 0.1 reshape.244
  33.0 0.1 copy.54
  33.1 0.1 lt.73
  33.2 0.1 reshape.184
  33.3 0.1 compare_and_fusion
  33.4 4.9 fusion.17
  38.3 0.1 copy.58
  38.4 0.1 copy.57
  38.5 0.1 copy.62
  38.6 0.1 select_reduce_fusion
  38.7 0.1 copy.63
  38.8 0.1 reshape.204
  39.0 8.3 gather_fusion.3
  47.3 13.3 %all-to-all-start.1 = ((bf16[64,2,64,768]{3,2,1,0:T(8,128)(2,1)}), bf16[64,2,64,768]{3,2,1,0:T(8,128)(2,1)}, u32[]{:S(2)}, u32[]{:S(2)}) async-start(bf16[64,2,64,768]{3,2,1,0:T(8,128)(2,1)} %bitcast.68), calls=%async_computation.1 | async-start | bytes 25165824 | tf_op jit(solution)/shard_map/all_to_all | solution.py:56
  60.6 8.3 gather_fusion.1
  68.9 263.8 %all-to-all-done.1 = bf16[64,2,64,768]{3,2,1,0:T(8,128)(2,1)} async-done(((bf16[64,2,64,768]{3,2,1,0:T(8,128)(2,1)}), bf16[64,2,64,768]{3,2,1,0:T(8,128)(2,1)}, u32[]{:S(2)}, u32[]{:S(2)}) %all-to-all-start.1) | async-done | bytes 12582944 | tf_op jit(solution)/shard_map/all_to_all | solution.py:56
  332.7 14.5 %all-to-all-start = ((bf16[64,2,64,768]{3,2,1,0:T(8,128)(2,1)}), bf16[64,2,64,768]{3,2,1,0:T(8,128)(2,1)}, u32[]{:S(2)}, u32[]{:S(2)}) async-start(bf16[64,2,64,768]{3,2,1,0:T(8,128)(2,1)} %bitcast.67), calls=%async_computation | async-start | bytes 25165824 | tf_op jit(solution)/shard_map/all_to_all | solution.py:57
  347.2 0.8 copy.91
  348.0 0.2 dynamic-slice_reduce_fusion
  348.2 0.1 reshape.188
  348.3 0.1 broadcast_in_dim.41
  348.4 0.1 broadcast_in_dim.42
  348.5 0.2 add_reduce_fusion
  348.7 272.2 %all-to-all-done = bf16[64,2,64,768]{3,2,1,0:T(8,128)(2,1)} async-done(((bf16[64,2,64,768]{3,2,1,0:T(8,128)(2,1)}), bf16[64,2,64,768]{3,2,1,0:T(8,128)(2,1)}, u32[]{:S(2)}, u32[]{:S(2)}) %all-to-all-start) | async-done | bytes 12582944 | tf_op jit(solution)/shard_map/all_to_all | solution.py:57
  620.8 4.0 all-to-all-start.2
  624.9 12.0 %gather_fusion.4 = bf16[96,64,768]{2,1,0:T(8,128)(2,1)} fusion(bf16[128,64,768]{2,1,0:T(8,128)(2,1)} %bitcast.12, s32[1024]{0:T(1024)S(1)} %pad_clamp_fusion), kind=kCustom, calls=%fused_computation.4 | custom fusion | bytes 18874752 | tf_op jit(solution)/shard_map/gather | solution.py:50
  636.9 20.2 %reshape.191 = bf16[4,1536,6,128]{3,2,1,0:T(8,128)(2,1)} reshape(bf16[96,64,768]{2,1,0:T(8,128)(2,1)} %gather_fusion.4) | data formatting | bytes 18874368 | tf_op jit(solution)/shard_map/reshape | solution.py:51
  657.1 12.0 %gather_fusion.2 = bf16[96,64,768]{2,1,0:T(8,128)(2,1)} fusion(bf16[128,64,768]{2,1,0:T(8,128)(2,1)} %bitcast.8, s32[1024]{0:T(1024)S(1)} %pad_clamp_fusion), kind=kCustom, calls=%fused_computation.2 | custom fusion | bytes 18874752 | tf_op jit(solution)/shard_map/gather | solution.py:50
  669.1 20.2 %reshape.187 = bf16[4,1536,6,128]{3,2,1,0:T(8,128)(2,1)} reshape(bf16[96,64,768]{2,1,0:T(8,128)(2,1)} %gather_fusion.2) | data formatting | bytes 18874368 | tf_op jit(solution)/shard_map/reshape | solution.py:51
  689.2 11.5 %fusion.6 = f32[4,6,1536,64]{2,3,1,0:T(8,128)} fusion(bf16[4,1536,6,128]{3,2,1,0:T(8,128)(2,1)} %reshape.191, bf16[64,4,768]{2,0,1:T(8,128)(2,1)S(1)} %all-to-all-done.2), kind=kOutput, calls=%fused_computation.13 | convolution fusion | flops 603979776 | bytes 19267584 | tf_op jit(solution)/shard_map/rqhd,rkhd->rhqk/dot_general | solution.py:59
  700.8 10.0 %fusion.45 = (f32[4,6,64]{2,1,0:T(8,128)S(1)}, bf16[4,6,64,1536]{3,2,1,0:T(8,128)(2,1)S(1)}) fusion(f32[4,6,1536,64]{2,3,1,0:T(8,128)} %fusion.6, pred[4,1536]{1,0:T(4,128)(4,1)S(1)} %broadcast_in_dim.42), kind=kOutput, calls=%fused_computation.61 | output fusion | flops 18875904 | bytes 14168064 | tf_op jit(solution)/shard_map/sub | solution.py:64
  710.8 7.5 fusion.32
  718.3 0.3 copy.68
  718.6 4.0 convolution_convert_fusion
  722.7 0.0 all-gather.3.cloned.1.call-update
  722.7 0.0 copy-start.1
  722.7 124.1 %all-gather.3.cloned.1.call-done = bf16[1024,6144]{1,0:T(8,128)(2,1)} async-done(((bf16[256,6144]{1,0:T(8,128)(2,1)}), bf16[1024,6144]{1,0:T(8,128)(2,1)}) %all-gather.3.cloned.1.call-update) | async-done | bytes 12582928 | tf_op jit(solution)/shard_map/all_gather | solution.py:74
  846.8 9.5 %reduce_sum.45 = bf16[256,6144]{1,0:T(8,128)(2,1)} reduce(bf16[4,256,6144]{2,1,0:T(8,128)(2,1)} %bitcast.69, bf16[]{:T(256)} %constant.66.clone.1), dimensions={0}, to_apply=%region_5.6 | reduce | flops 4718592 | bytes 15728642 | tf_op jit(solution)/shard_map/reduce_sum | solution.py:74
  856.3 2.1 convert_convert_fusion
  (30 shorter events, 0.1 us)
Async XLA Ops:
  6.5 32.5 %copy-start = (bf16[768,768]{1,0:T(8,128)(2,1)S(1)}, bf16[768,768]{1,0:T(8,128)(2,1)}, u32[]{:S(2)}) copy-start(bf16[768,768]{1,0:T(8,128)(2,1)} %param.8) | copy-start | bytes 3538948
  6.5 1.2 copy-start.2
  7.7 25.5 %copy-start.5 = (s32[256]{0:T(256)S(1)}, s32[256]{0:T(256)}, u32[]{:S(2)}) copy-start(s32[256]{0:T(256)} %param.12) | copy-start | bytes 3076
  47.3 13.4 %copy-start.3 = (bf16[768,768]{1,0:T(8,128)(2,1)S(1)}, bf16[768,768]{1,0:T(8,128)(2,1)}, u32[]{:S(2)}) copy-start(bf16[768,768]{1,0:T(8,128)(2,1)} %param.9) | copy-start | bytes 3538948
  47.3 285.5 %all-to-all-start.1 = ((bf16[64,2,64,768]{3,2,1,0:T(8,128)(2,1)}), bf16[64,2,64,768]{3,2,1,0:T(8,128)(2,1)}, u32[]{:S(2)}, u32[]{:S(2)}) async-start(bf16[64,2,64,768]{3,2,1,0:T(8,128)(2,1)} %bitcast.68), calls=%async_computation.1 | async-start | bytes 25165824 | tf_op jit(solution)/shard_map/all_to_all | solution.py:56
  332.7 14.5 %copy-start.4 = (bf16[64,3072]{1,0:T(8,128)(2,1)S(1)}, bf16[64,3072]{1,0:T(8,128)(2,1)}, u32[]{:S(2)}) copy-start(bf16[64,3072]{1,0:T(8,128)(2,1)} %param.7) | copy-start | bytes 1179652
  332.7 288.1 %all-to-all-start = ((bf16[64,2,64,768]{3,2,1,0:T(8,128)(2,1)}), bf16[64,2,64,768]{3,2,1,0:T(8,128)(2,1)}, u32[]{:S(2)}, u32[]{:S(2)}) async-start(bf16[64,2,64,768]{3,2,1,0:T(8,128)(2,1)} %bitcast.67), calls=%async_computation | async-start | bytes 25165824 | tf_op jit(solution)/shard_map/all_to_all | solution.py:57
  620.8 68.4 %all-to-all-start.2 = ((bf16[64,4,768]{2,0,1:T(8,128)(2,1)}), bf16[64,4,768]{2,0,1:T(8,128)(2,1)S(1)}, u32[]{:S(2)}, u32[]{:S(2)}) async-start(bf16[64,4,768]{2,0,1:T(8,128)(2,1)} %bitcast.64), calls=%async_computation.2 | async-start | bytes 786432 | tf_op jit(solution)/shard_map/all_to_all | solution.py:20
  624.8 222.0 %all-gather.3.cloned.1.call-start = ((), (), s32[]{:S(2)}) async-start(), calls=%async_computation.3 | async-start | bytes 15728640 | tf_op jit(solution)/shard_map/all_gather | solution.py:74
  700.8 17.8 %slice-start = ((s8[9437184]{0:T(1024)(128)(4,1)}), s8[1048576]{0:T(1024)(128)(4,1)S(1)}, s32[]{:S(2)}) async-start(s8[9437184]{0:T(1024)(128)(4,1)} %bitcast.73), calls=%async_computation.4 | async-start | bytes 2097152
  700.8 17.8 %slice-start.1 = ((s8[9437184]{0:T(1024)(128)(4,1)}), s8[4194304]{0:T(1024)(128)(4,1)S(1)}, s32[]{:S(2)}) async-start(s8[9437184]{0:T(1024)(128)(4,1)} %bitcast.73), calls=%async_computation.5 | async-start | bytes 8388608
  710.8 7.8 slice-start.2
  722.7 135.7 %copy-start.1 = (bf16[768,768]{1,0:T(8,128)(2,1)S(1)}, bf16[768,768]{1,0:T(8,128)(2,1)}, u32[]{:S(2)}) copy-start(bf16[768,768]{1,0:T(8,128)(2,1)} %param.8) | copy-start | bytes 3538948
Sparse Core Ops, SparseCore 0:
  722.8 123.9 all-gather.2
